TPU v7x, 128 devices: a whole 4x4x4 slice. The times are simulated.
128 devices in a mesh: row: 8 (over z, core), col: 16 (over y, x).
Axes of the slice: x: 4, y: 4, z: 4, core: 2. Of those that a mesh axis runs over, the one named last changes fastest.
Arguments:
- singles: bfloat16 [1024, 384], P('row', 'col'), may hold values from -6 to 6
- pair_in: bfloat16 [1024, 1024, 128], P('row', 'col'), may hold values from -6 to 6
- proj_weight: bfloat16 [384, 256], P('col'), may hold values from -0.3125 to 0.3125
- gain_first: float32 [128], replicated, may hold values from 0.1 to 1.9
- first_in: bfloat16 [128, 1024], replicated, may hold values from -0.5 to 0.5
- first_out: bfloat16 [512, 128], replicated, may hold values from -0.25 to 0.25
- gain_second: float32 [128], replicated, may hold values from 0.1 to 1.9
- second_in: bfloat16 [128, 1024], replicated, may hold values from -0.5 to 0.5
- second_out: bfloat16 [512, 128], replicated, may hold values from -0.25 to 0.25
- head_weight: bfloat16 [128, 64], replicated, may hold values from -1.5 to 1.5
- pae_bins: int32 [1024, 1024], P('row', 'col'), may hold values from 0 to 63
- chain_perm: int32 [1024], replicated, may hold values from 0 to 1023, as said below
- resolved_counts: int32 [8, 16], P('row'), may hold values from 1 to 256, 2048 in all within a row
- tile_order: int32 [8, 4096], P('row', 'col'), may hold values from 0 to 255, as said below
Outputs:
- pair_grad: bfloat16 [1024, 1024, 128], P('row', 'col')
- single_grad: float32 [1024, 384], P('row', 'col')
- second_in_grad: float32 [128, 1024], replicated
- second_out_grad: float32 [512, 128], replicated
- head_grad: float32 [128, 64], replicated
Inputs may be any that keep to these rules, and one draw needn't show every extreme that they name: chain_perm maps every aligned group of 64 tokens onto itself, moving whole aligned runs of 16 tokens and keeping the order inside a run. Each row of resolved_counts sums to 2048, and its largest entry is 256. In each row of tile_order, entries b * 256 to (b + 1) * 256 - 1 are a permutation of 0 to 255.
All inputs are finite; a program needn't handle non-finite values.
Results may differ from a plain program's by a relative error of at most 0.011.
Values may be sent and summed in bfloat16 or wider, within the bound.
A program may use at most 64 MiB of HBM per device.

v0:
```python
import jax
import jax.numpy as jnp
from jax import lax
from jax.sharding import PartitionSpec as P

TILE = 32


def contract(left_op, right_op, left_dim, right_dim):
    return lax.dot_general(
        left_op,
        right_op,
        (((left_dim,), (right_dim,)), ((), ())),
        preferred_element_type=jnp.float32,
    )


def block_size(extent, per_item, limit):
    best = 1
    for candidate in range(1, extent + 1):
        if extent % candidate == 0 and candidate * per_item <= limit:
            best = candidate
    return best


def transition_forward(start_z, gain_vec, w_in, w_out):
    hidden_units = w_out.shape[0]
    average = jnp.mean(start_z, axis=-1, keepdims=True)
    centred = start_z - average
    scaling = lax.rsqrt(jnp.mean(centred * centred, axis=-1, keepdims=True) + 1e-05)
    normed = centred * scaling
    inputs = (normed * gain_vec).astype(jnp.bfloat16)
    gate_up = jnp.dot(inputs, w_in, preferred_element_type=jnp.float32)
    gate_part = gate_up[:, :hidden_units]
    up_part = gate_up[:, hidden_units:]
    gate_sig = jax.nn.sigmoid(gate_part)
    hidden_act = (gate_part * gate_sig * up_part).astype(jnp.bfloat16)
    result = jnp.dot(hidden_act, w_out, preferred_element_type=jnp.float32)
    return (result, (normed, scaling, inputs, gate_part, up_part, gate_sig, hidden_act))


def transition_backward(saved, grad_out, gain_vec, w_in, w_out, with_weights):
    normed, scaling, inputs, gate_part, up_part, gate_sig, hidden_act = saved
    grad_hidden = contract(grad_out, w_out, 1, 1)
    grad_gate = grad_hidden * up_part * gate_sig * (1.0 + gate_part * (1.0 - gate_sig))
    grad_up = grad_hidden * gate_part * gate_sig
    grad_both = jnp.concatenate([grad_gate, grad_up], axis=1).astype(jnp.bfloat16)
    grad_normed = contract(grad_both, w_in, 1, 1) * gain_vec
    grad_field = scaling * (
        grad_normed
        - jnp.mean(grad_normed, axis=-1, keepdims=True)
        - normed * jnp.mean(grad_normed * normed, axis=-1, keepdims=True)
    )
    if with_weights:
        return (grad_field, contract(inputs, grad_both, 0, 0), contract(hidden_act, grad_out, 0, 0))
    return (grad_field, None, None)


def head_step(rounded_z, targets, keep_mask, head_weight):
    logits = jnp.dot(rounded_z, head_weight, preferred_element_type=jnp.float32)
    exponent = jnp.exp(logits - jnp.max(logits, axis=-1, keepdims=True))
    probability = exponent / jnp.sum(exponent, axis=-1, keepdims=True)
    onehot = (targets[:, None] == lax.broadcasted_iota(jnp.int32, logits.shape, 1)).astype(
        jnp.float32
    )
    grad_logits = ((probability - onehot) * keep_mask[:, None]).astype(jnp.bfloat16)
    return (
        contract(grad_logits, head_weight, 1, 1).astype(jnp.bfloat16),
        contract(rounded_z, grad_logits, 0, 0),
    )


def second_step(pair_one, targets, live_mask, gain_second, second_in, second_out, head_weight):
    start_f = pair_one.astype(jnp.float32)
    delta, saved = transition_forward(start_f, gain_second, second_in, second_out)
    rounded_z = (start_f + live_mask[:, None] * delta).astype(jnp.bfloat16)
    grad_two, head_part = head_step(rounded_z, targets, jnp.ones_like(live_mask), head_weight)
    masked_out = jnp.where(live_mask[:, None] > 0, grad_two, jnp.zeros((), jnp.bfloat16))
    back_field, in_part, out_part = transition_backward(
        saved, masked_out, gain_second, second_in, second_out, True
    )
    return (
        (grad_two.astype(jnp.float32) + back_field).astype(jnp.bfloat16),
        in_part,
        out_part,
        head_part,
    )


def local(
    singles,
    pair_in,
    proj_weight,
    gain_first,
    first_in,
    first_out,
    gain_second,
    second_in,
    second_out,
    head_weight,
    pae_bins,
    chain_perm,
    resolved_counts,
    tile_order,
):
    rows_dev, cols_dev, width = pair_in.shape
    tile_len = TILE
    tiles_dev = rows_dev * cols_dev // tile_len
    token_count = chain_perm.shape[0]
    row_index = lax.axis_index("row")
    col_index = lax.axis_index("col")
    col_count = lax.axis_size("col")
    partial_proj = jnp.dot(singles, proj_weight, preferred_element_type=jnp.float32)
    projected = lax.psum(partial_proj, "col")
    left_part = projected[:, :width]
    right_part = projected[:, width:].astype(jnp.bfloat16)
    col_start = col_index * cols_dev
    right_all = lax.all_gather(right_part, "row", axis=0, tiled=True)
    col_right = lax.dynamic_slice_in_dim(right_all, col_start, cols_dev, 0)
    col_right_f = col_right.astype(jnp.float32)
    block_rows = block_size(rows_dev, cols_dev, 1024)
    row_blocks = rows_dev // block_rows
    block_pairs = block_rows * cols_dev

    def start_field(block_index):
        first_row = block_index * block_rows
        pair_rows = lax.dynamic_slice_in_dim(pair_in, first_row, block_rows, 0).astype(jnp.float32)
        left_rows = lax.dynamic_slice_in_dim(left_part, first_row, block_rows, 0)
        field_rows = pair_rows + left_rows[:, None, :] + col_right_f[None, :, :]
        return field_rows.reshape(block_pairs, width)

    def forward_block(block_index):
        start_z = start_field(block_index)
        delta, unused_saved = transition_forward(start_z, gain_first, first_in, first_out)
        return (start_z + delta).astype(jnp.bfloat16)

    block_ids = jnp.arange(row_blocks, dtype=jnp.int32)
    pair_one = lax.map(forward_block, block_ids).reshape(rows_dev * cols_dev, width)
    live_count = resolved_counts[0, col_index]
    order_list = tile_order[0]
    tile_iota = jnp.arange(tiles_dev, dtype=jnp.int32)
    rank_of = jnp.sum(
        jnp.where(order_list[None, :] == tile_iota[:, None], tile_iota[None, :], 0), axis=1
    )
    tile_live = rank_of < live_count
    pair_live = jnp.repeat(tile_live, tile_len).astype(jnp.float32)
    perm_rows = (
        lax.dynamic_slice_in_dim(chain_perm, row_index * rows_dev, rows_dev, 0)
        - row_index * rows_dev
    )
    perm_cols = lax.dynamic_slice_in_dim(chain_perm, col_start, cols_dev, 0) - col_start
    targets = jnp.take(jnp.take(pae_bins, perm_rows, axis=0), perm_cols, axis=1).reshape(
        rows_dev * cols_dev
    )
    pair_stack = pair_one.reshape(row_blocks, block_pairs, width)
    target_stack = targets.reshape(row_blocks, block_pairs)
    live_stack = pair_live.reshape(row_blocks, block_pairs)
    zero_in = jnp.zeros(second_in.shape, jnp.float32)
    zero_out = jnp.zeros(second_out.shape, jnp.float32)
    zero_head = jnp.zeros(head_weight.shape, jnp.float32)

    def head_block(running, operands):
        grad_two, head_part = head_step(operands[0], operands[1], 1.0 - operands[2], head_weight)
        return (running + head_part, grad_two)

    head_sum, rest_stack = lax.scan(head_block, zero_head, (pair_stack, target_stack, live_stack))
    rest_tiles = rest_stack.reshape(tiles_dev, tile_len, width)
    slots = -(-tiles_dev // col_count)
    row_counts = resolved_counts[0]
    offsets = jnp.cumsum(row_counts) - row_counts
    my_offset = offsets[col_index]
    worker_iota = jnp.arange(col_count, dtype=jnp.int32)[:, None]
    slot_iota = jnp.arange(slots, dtype=jnp.int32)[None, :]
    send_rank = col_count * slot_iota + jnp.mod(worker_iota - my_offset, col_count)
    send_valid = send_rank < live_count
    send_ids = order_list[jnp.minimum(send_rank, tiles_dev - 1)]
    tile_view = pair_one.reshape(tiles_dev, tile_len, width)
    target_view = targets.reshape(tiles_dev, tile_len).astype(jnp.bfloat16)
    send_pairs = jnp.where(
        send_valid[:, :, None, None], tile_view[send_ids], jnp.zeros((), jnp.bfloat16)
    )
    send_targets = jnp.where(
        send_valid[:, :, None], target_view[send_ids], jnp.zeros((), jnp.bfloat16)
    )
    recv_pairs, recv_targets = (
        lax.all_to_all(send_pairs, "col", split_axis=0, concat_axis=0, tiled=True),
        lax.all_to_all(send_targets, "col", split_axis=0, concat_axis=0, tiled=True),
    )
    work_count = tiles_dev // 2
    position = jnp.arange(work_count, dtype=jnp.int32)
    global_rank = col_count * position + col_index
    source = jnp.sum((offsets[None, :] <= global_rank[:, None]).astype(jnp.int32), axis=1) - 1
    source_slot = (global_rank - offsets[source]) // col_count
    flat_index = source * slots + source_slot
    work_pairs = recv_pairs.reshape(col_count * slots, tile_len, width)[flat_index]
    work_targets = recv_targets.reshape(col_count * slots, tile_len)[flat_index].astype(jnp.int32)
    block_tiles = block_size(work_count, tile_len, 1024)
    work_blocks = work_count // block_tiles
    work_pair_stack = work_pairs.reshape(work_blocks, block_tiles * tile_len, width)
    work_target_stack = work_targets.reshape(work_blocks, block_tiles * tile_len)

    def worker_block(running, operands):
        all_live = jnp.ones(operands[1].shape, jnp.float32)
        grad_one, in_part, out_part, head_part = second_step(
            operands[0], operands[1], all_live, gain_second, second_in, second_out, head_weight
        )
        return ((running[0] + in_part, running[1] + out_part, running[2] + head_part), grad_one)

    weight_sums, work_grad_stack = lax.scan(
        worker_block, (zero_in, zero_out, head_sum), (work_pair_stack, work_target_stack)
    )
    work_grads = work_grad_stack.reshape(work_count, tile_len, width)
    back_rank = col_count * slot_iota + jnp.mod(col_index - offsets[:, None], col_count)
    back_valid = back_rank < row_counts[:, None]
    back_position = jnp.minimum((offsets[:, None] + back_rank) // col_count, work_count - 1)
    back_pairs = jnp.where(
        back_valid[:, :, None, None], work_grads[back_position], jnp.zeros((), jnp.bfloat16)
    )
    returned = lax.all_to_all(back_pairs, "col", split_axis=0, concat_axis=0, tiled=True)
    tile_worker = jnp.mod(my_offset + rank_of, col_count)
    tile_slot = jnp.minimum(rank_of // col_count, slots - 1)
    from_worker = returned.reshape(col_count * slots, tile_len, width)[
        tile_worker * slots + tile_slot
    ]
    grad_one_all = jnp.where(tile_live[:, None, None], from_worker, rest_tiles).reshape(
        rows_dev * cols_dev, width
    )
    grad_one_stack = grad_one_all.reshape(row_blocks, block_pairs, width)

    def backward_block(running, operands):
        block_index, grad_one = operands
        start_z = start_field(block_index)
        unused_delta, saved = transition_forward(start_z, gain_first, first_in, first_out)
        back_field, unused_in, unused_out = transition_backward(
            saved, grad_one, gain_first, first_in, first_out, False
        )
        grad_zero = (grad_one.astype(jnp.float32) + back_field).reshape(block_rows, cols_dev, width)
        return (
            running + jnp.sum(grad_zero, axis=0),
            (grad_zero.astype(jnp.bfloat16), jnp.sum(grad_zero, axis=1)),
        )

    right_grad, (pair_grad_stack, left_stack) = lax.scan(
        backward_block, jnp.zeros((cols_dev, width), jnp.float32), (block_ids, grad_one_stack)
    )
    pair_grad = pair_grad_stack.reshape(rows_dev, cols_dev, width)
    left_grad = left_stack.reshape(rows_dev, width)
    token_part = jnp.zeros((token_count, 2 * width), jnp.float32)
    token_part = lax.dynamic_update_slice(token_part, left_grad, (row_index * rows_dev, 0))
    token_part = lax.dynamic_update_slice(token_part, right_grad, (col_start, width))
    token_total, in_total, out_total, head_total = lax.psum(
        (token_part, weight_sums[0], weight_sums[1], weight_sums[2]), ("row", "col")
    )
    token_rows = lax.dynamic_slice_in_dim(token_total, row_index * rows_dev, rows_dev, 0).astype(
        jnp.bfloat16
    )
    single_grad = contract(token_rows, proj_weight, 1, 1)
    return (
        pair_grad,
        single_grad,
        in_total / token_count,
        out_total / token_count,
        head_total / token_count,
    )


def solution(mesh):
    in_specs = (
        P("row", "col"),
        P("row", "col", None),
        P("col", None),
        P(),
        P(),
        P(),
        P(),
        P(),
        P(),
        P(),
        P("row", "col"),
        P(),
        P("row", None),
        P("row", "col"),
    )
    out_specs = (P("row", "col", None), P("row", "col"), P(), P(), P())
    return jax.shard_map(local, mesh=mesh, in_specs=in_specs, out_specs=out_specs, check_vma=False)
```

profile of v0, /device:TPU:1, one launch (start us, length us, event | category | flops | bytes accessed | tf_op | source)
XLA Modules:
  0.0 618.8 jit_solution(7770418198475508663)
XLA Ops:
  7.9 1.5 fusion.87
  13.8 1.9 gather_fusion.2
  21.9 7.6 %all-to-all-start.1 = ((bf16[16,2,256]{2,1,0:T(2,128)(2,1)}), bf16[16,2,256]{2,1,0:T(2,128)(2,1)S(1)}, u32[]{:S(2)}, u32[]{:S(2)}) async-start(bf16[16,2,256]{2,1,0:T(2,128)(2,1)} %reshape.938), calls=%async_computation.1 | async-start | bytes 32768 | tf_op jit(solution)/shard_map/all_to_all | solution.py:187
  30.6 10.0 %fusion.77 = s32[128]{0:T(128)S(1)} fusion(s32[128]{0:T(128)S(1)} %convert_reduce_fusion.1, s32[]{:T(128)} %bitcast.33, s32[]{:T(128)} %bitcast.34, s32[]{:T(128)} %bitcast.35, s32[]{:T(128)} %bitcast.36, s32[]{:T(128)} %bitcast.37, s32[]{:T(128)} %bitcast.39, s32[]{:T(128)} %bitcast.38, s32[]{:T(128)} %bitcast.16, s32[]{:T(128)} %bitcast.18, s32[]{:T(128)} %bitcast.20, ...), kind=kLoop, calls=%fused_computation.208 | loop fusion | flops 7296 | bytes 1092 | tf_op jit(solution)/shard_map/select_n | solution.py:195
  42.0 54.0 %all-reduce.6.cloned.1.call-done = f32[128,256]{1,0:T(8,128)} async-done(((f32[128,256]{1,0:T(8,128)}), f32[128,256]{1,0:T(8,128)}) %all-reduce.6.cloned.1.call-update) | async-done | bytes 131088 | tf_op jit(solution)/shard_map/psum | solution.py:114
  96.8 15.6 %all_gather.3 = bf16[1024,128]{1,0:T(8,128)(2,1)S(1)} all-gather(bf16[128,128]{1,0:T(8,128)(2,1)S(1)} %slice.95), channel_id=1, replica_groups=mesh['row'=8,'col'=16] {'row'}, dimensions={0}, use_global_device_ids=true | all-gather | bytes 294912 | tf_op jit(solution)/shard_map/all_gather | solution.py:118
  112.5 1.5 slice.72
  113.9 1.6 broadcast.784.clone
  115.5 64.0 %while.55 = (s32[]{:T(128)}, bf16[8,1024,128]{2,1,0:T(8,128)(2,1)}, s32[8]{0:T(128)S(1)}, bf16[128,64,128]{2,1,0:T(8,128)(2,1)}, f32[128,128]{1,0:T(8,128)}, /*i...) while((s32[]{:T(128)}, bf16[8,1024,128]{2,1,0:T(8,128)(2,1)}, ...), condition=%wide.region_6.7_spmd, body=%wide.region_3.6_spmd.sunk | while | flops 407897088 | bytes 11818179 | solution.py:138
  118.7 1.4 multiply_reduce_fusion.5
  121.2 2.3 fusion.163
  126.7 1.4 multiply_reduce_fusion.5
  129.2 2.3 fusion.163
  134.7 1.4 multiply_reduce_fusion.5
  137.2 2.3 fusion.163
  142.7 1.4 multiply_reduce_fusion.5
  145.2 2.3 fusion.163
  153.2 2.3 fusion.163
  158.7 1.4 multiply_reduce_fusion.5
  161.2 2.3 fusion.163
  166.7 1.4 multiply_reduce_fusion.5
  169.2 2.3 fusion.163
  177.2 2.3 fusion.163
  179.6 2.6 gather_fusion.3
  182.2 1.6 broadcast_select_fusion
  183.7 4.8 all-to-all-start
  189.2 22.2 %while.56 = (s32[]{:T(128)}, f32[128,64]{0,1:T(8,128)S(1)}, bf16[8,1024,128]{2,1,0:T(8,128)(2,1)S(1)}, bf16[8,1024,128]{2,1,0:T(8,128)(2,1)}, bf16[128,64]{0,1:T...) while((s32[]{:T(128)}, f32[128,64]{0,1:T(8,128)S(1)}, ...), condition=%wide.region_10.11_spmd.clone, body=%wide.region_7.10_spmd.clone.sunk | while | flops 51592192 | bytes 1995891 | solution.py:166
  211.5 9.9 %all-to-all-done = bf16[16,16,32,128]{3,2,1,0:T(8,128)(2,1)} async-done(((bf16[16,16,32,128]{3,2,1,0:T(8,128)(2,1)}), bf16[16,16,32,128]{3,2,1,0:T(8,128)(2,1)}, u32[]{:S(2)}, u32[]{:S(2)}) %all-to-all-start) | async-done | bytes 2097184 | tf_op jit(solution)/shard_map/all_to_all | solution.py:186
  221.4 2.4 gather_fusion.4
  223.8 45.5 %while.57 = (s32[]{:T(128)}, f32[128,1024]{1,0:T(8,128)}, f32[512,128]{1,0:T(8,128)S(1)}, f32[128,64]{0,1:T(8,128)S(1)}, bf16[4,1024,128]{2,1,0:T(8,128)(2,1)}, ...) while((s32[]{:T(128)}, f32[128,1024]{1,0:T(8,128)}, ...), condition=%wide.region_19.20_spmd.clone, body=%wide.region_12.19_spmd.clone.sunk | while | flops 1282874368 | bytes 39037144 | solution.py:209
  231.5 3.5 fusion.189
  242.8 3.7 fusion.189
  254.2 3.7 fusion.189
  265.6 3.7 fusion.189
  269.3 2.3 gather_fusion.7
  271.6 1.5 broadcast_select_fusion.1
  273.2 3.7 all-to-all-start.2
  278.3 161.1 %all-reduce.8.cloned.1.call-done = (f32[128,1024]{1,0:T(8,128)}, f32[512,128]{1,0:T(8,128)}) async-done(((f32[128,1024]{1,0:T(8,128)}, f32[512,128]{1,0:T(8,128)}), (f32[128,1024]{1,0:T(8,128)}, f32[512,128]{1,0:T(8,128)})) %all-reduce.8.cloned.1.call-update) | async-done | bytes 786448 | tf_op jit(solution)/shard_map/psum | solution.py:251
  439.5 1.7 broadcast_multiply_fusion.8
  441.1 1.9 broadcast_multiply_fusion.7
  443.0 2.2 gather_fusion.8
  445.2 3.6 bitcast_select_fusion
  448.7 89.8 %while.58 = (s32[]{:T(128)}, f32[64,128]{1,0:T(8,128)S(1)}, bf16[8,16,64,128]{3,2,1,0:T(8,128)(2,1)}, f32[8,16,128]{2,1,0:T(8,128)}, bf16[8,1024,128]{2,1,0:T(8,...) while((s32[]{:T(128)}, f32[64,128]{1,0:T(8,128)S(1)}, ...), condition=%wide.region_27.28_spmd.clone, body=%wide.region_20.27_spmd.clone.sunk | while | flops 686169088 | bytes 20674808 | solution.py:243
  454.5 2.0 fusion.198
  456.5 1.4 fusion.199
  465.7 2.0 fusion.198
  467.8 1.4 fusion.199
  474.3 1.4 multiply_reduce_fusion.6
  476.9 2.0 fusion.198
  479.0 1.4 fusion.199
  485.5 1.4 multiply_reduce_fusion.6
  488.2 2.0 fusion.198
  490.2 1.4 fusion.199
  499.4 2.0 fusion.198
  501.4 1.4 fusion.199
  508.0 1.4 multiply_reduce_fusion.6
  510.6 2.0 fusion.198
  512.7 1.4 fusion.199
  521.8 2.0 fusion.198
  523.9 1.4 fusion.199
  530.4 1.4 multiply_reduce_fusion.6
  533.0 2.0 fusion.198
  535.1 1.4 fusion.199
  539.5 71.1 %all-reduce.9 = (bf16[1024,256]{1,0:T(8,128)(2,1)S(1)}, f32[128,64]{0,1:T(8,128)S(1)}) all-reduce(f32[1024,256]{1,0:T(8,128)S(1)} %constant_dynamic-update-slice_fusion.2, f32[128,64]{0,1:T(8,128)S(1)} %get-tuple-element.223), channel_id=1, replica_groups=mesh['row'=8,'col'=16] {'row','col'}, use_global_device_ids=true, to_apply=%region_28.29 | all-reduce | flops 270336 | bytes 1638400 | tf_op jit(solution)/shard_map/psum | solution.py:251
  (440 shorter events, 153.7 us)
Async XLA Ops:
  7.2 0.7 copy-start
  7.2 6.6 %copy-start.1 = (s32[1,256]{1,0:T(1,128)S(1)}, s32[1,256]{1,0:T(1,128)}, u32[]{:S(2)}) copy-start(s32[1,256]{1,0:T(1,128)} %param.35) | copy-start | bytes 3076
  7.2 88.8 %all-reduce.6.cloned.1.call-start = ((), (), s32[]{:S(2)}) async-start(), calls=%async_computation.3 | async-start | bytes 262144 | tf_op jit(solution)/shard_map/psum | solution.py:114
  13.8 3.7 copy-start.9
  13.8 5.6 copy-start.11
  20.2 95.3 %copy-start.2 = (bf16[128,1024]{1,0:T(8,128)(2,1)S(1)}, bf16[128,1024]{1,0:T(8,128)(2,1)}, u32[]{:S(2)}) copy-start(bf16[128,1024]{1,0:T(8,128)(2,1)} %param.26) | copy-start | bytes 786436
  20.2 95.3 %copy-start.8 = (f32[128]{0:T(128)S(1)}, f32[128]{0:T(128)}, u32[]{:S(2)}) copy-start(f32[128]{0:T(128)} %param.25) | copy-start | bytes 1540
  21.9 19.1 %all-to-all-start.1 = ((bf16[16,2,256]{2,1,0:T(2,128)(2,1)}), bf16[16,2,256]{2,1,0:T(2,128)(2,1)S(1)}, u32[]{:S(2)}, u32[]{:S(2)}) async-start(bf16[16,2,256]{2,1,0:T(2,128)(2,1)} %reshape.938), calls=%async_computation.1 | async-start | bytes 32768 | tf_op jit(solution)/shard_map/all_to_all | solution.py:187
  183.7 37.7 %all-to-all-start = ((bf16[16,16,32,128]{3,2,1,0:T(8,128)(2,1)}), bf16[16,16,32,128]{3,2,1,0:T(8,128)(2,1)}, u32[]{:S(2)}, u32[]{:S(2)}) async-start(bf16[16,16,32,128]{3,2,1,0:T(8,128)(2,1)} %broadcast_select_fusion), calls=%async_computation | async-start | bytes 4194304 | tf_op jit(solution)/shard_map/all_to_all | solution.py:186
  188.5 0.7 copy-start.7
  211.4 10.0 %copy-start.4 = (bf16[8,1024,128]{2,1,0:T(8,128)(2,1)}, bf16[8,1024,128]{2,1,0:T(8,128)(2,1)S(1)}, u32[]{:S(2)}) copy-start(bf16[8,1024,128]{2,1,0:T(8,128)(2,1)S(1)} %get-tuple-element.217) | copy-start | bytes 6291460
  211.4 12.3 %copy-start.5 = (bf16[128,1024]{1,0:T(8,128)(2,1)S(1)}, bf16[128,1024]{1,0:T(8,128)(2,1)}, u32[]{:S(2)}) copy-start(bf16[128,1024]{1,0:T(8,128)(2,1)} %param.29) | copy-start | bytes 786436
  211.4 12.3 %copy-start.6 = (bf16[512,128]{1,0:T(8,128)(2,1)S(1)}, bf16[512,128]{1,0:T(8,128)(2,1)}, u32[]{:S(2)}) copy-start(bf16[512,128]{1,0:T(8,128)(2,1)} %param.30) | copy-start | bytes 393220
  211.4 12.3 %copy-start.10 = (f32[128]{0:T(128)S(1)}, f32[128]{0:T(128)}, u32[]{:S(2)}) copy-start(f32[128]{0:T(128)} %param.28) | copy-start | bytes 1540
  228.1 1.4 copy-start.12
  228.1 1.4 copy-start.13
  239.4 1.4 copy-start.12
  239.4 1.4 copy-start.13
  250.8 1.4 copy-start.12
  250.8 1.4 copy-start.13
  262.2 1.4 copy-start.12
  262.2 1.4 copy-start.13
  269.3 2.3 copy-start.3
  273.2 169.8 %all-to-all-start.2 = ((bf16[16,16,32,128]{3,2,1,0:T(8,128)(2,1)}), bf16[16,16,32,128]{3,2,1,0:T(8,128)(2,1)S(1)}, u32[]{:S(2)}, u32[]{:S(2)}) async-start(bf16[16,16,32,128]{3,2,1,0:T(8,128)(2,1)} %broadcast_select_fusion.1), calls=%async_computation.2 | async-start | bytes 4194304 | tf_op jit(solution)/shard_map/all_to_all | solution.py:219
  276.9 162.6 %all-reduce.8.cloned.1.call-start = ((), (), s32[]{:S(2)}) async-start(), calls=%async_computation.4 | async-start | bytes 1572864 | tf_op jit(solution)/shard_map/psum | solution.py:251
Sparse Core Ops, SparseCore 0:
  11.8 84.1 all-reduce.5
  283.0 156.3 all-reduce.7
where the time goes:
time: 623 us; the launch traced here: 619 us
  waiting for transfers between devices  226 us (36%)
  matrix products  115 us (18%)
  other arithmetic  88.6 us (14%)
  blocking collectives  86.8 us (14%)
  local copies, waits for them, and re-layouts  58.9 us (9%)
  starting transfers between devices  16.4 us (3%)
  between operations  14.5 us (2%)
  loops' own time  12.6 us (2%)
    psum x1, waiting for transfers between devices, local(): lax.psum((token_part, weight_sums[0], weight_sums[1], weight_sums[2]), ('...  161 us
    psum x1, blocking collectives, local(): lax.psum((token_part, weight_sums[0], weight_sums[1], weight_sums[2]), ('...  71.1 us
    dot_general x57, matrix products, contract(): lax.dot_general(left_op, right_op, (((left_dim,), (right_dim,)), ((), ())...  68 us
    psum x1, waiting for transfers between devices, local(): projected = lax.psum(partial_proj, 'col')  54 us
    reduce_sum x20, other arithmetic, transition_forward(): jnp.mean(centred * centred, axis=-1, keepdims=True) + 1e-05  23.1 us
    dot_general x12, matrix products, transition_forward(): result = jnp.dot(hidden_act, w_out, preferred_element_type=jnp.float32)  20.6 us
    reduce_sum x20, other arithmetic, transition_forward(): average = jnp.mean(start_z, axis=-1, keepdims=True)  19.2 us
    all_gather x1, blocking collectives, local(): right_all = lax.all_gather(right_part, 'row', axis=0, tiled=True)  15.6 us
  transfers between devices with their start and end apart: 5, of which 3 were waited for; matrix products, arithmetic and copies ran while one was open for 8% of the time, Pallas kernels for 0%

commit v1 on v0

--- a/solution.py
+++ b/solution.py
@@ -2,6 +2,7 @@
 import jax.numpy as jnp
 from jax import lax
 from jax.sharding import PartitionSpec as P
+from jax.lax import psum
 
 TILE = 32
 
@@ -103,6 +104,12 @@
     resolved_counts,
     tile_order,
 ):
+
+    def shape_the_masks(shard_axis, which_axis, page):
+        for k in (which_axis, shard_axis):
+            page = psum(page, k)
+        return page
+
     rows_dev, cols_dev, width = pair_in.shape
     tile_len = TILE
     tiles_dev = rows_dev * cols_dev // tile_len
@@ -248,8 +255,8 @@
     token_part = jnp.zeros((token_count, 2 * width), jnp.float32)
     token_part = lax.dynamic_update_slice(token_part, left_grad, (row_index * rows_dev, 0))
     token_part = lax.dynamic_update_slice(token_part, right_grad, (col_start, width))
-    token_total, in_total, out_total, head_total = lax.psum(
-        (token_part, weight_sums[0], weight_sums[1], weight_sums[2]), ("row", "col")
+    token_total, in_total, out_total, head_total = shape_the_masks(
+        "row", "col", (token_part, weight_sums[0], weight_sums[1], weight_sums[2])
     )
     token_rows = lax.dynamic_slice_in_dim(token_total, row_index * rows_dev, rows_dev, 0).astype(
         jnp.bfloat16

time: 623 us -> 571 us (0.917)
  waiting for transfers between devices: 226 us -> 133 us
  blocking collectives: 86.8 us -> 126 us
    psum x1 -> x2, waiting for transfers between devices: 161 us -> 39.8 us  [shape_the_masks(): page = psum(page, k)]
    psum x1 -> x2, blocking collectives: 71.1 us -> 110 us  [shape_the_masks(): page = psum(page, k)]
    all_to_all x1, waiting for transfers between devices: 0.01 us -> 28.7 us  [local(): lax.all_to_all(back_pairs, 'col', split_axis=0, concat_axis=0, tiled=True)]
  transfers between devices with their start and end apart: 5 -> 6, of which waited for: 3 -> 5; matrix products, arithmetic and copies ran while one was open for 8% -> 9% of each run, Pallas kernels for 0% -> 0%
where the time goes in v1:
time: 571 us; the launch traced here: 566 us
  waiting for transfers between devices  133 us (23%)
  blocking collectives  126 us (22%)
  matrix products  116 us (20%)
  other arithmetic  88.6 us (16%)
  local copies, waits for them, and re-layouts  60 us (11%)
  starting transfers between devices  16.4 us (3%)
  between operations  14.2 us (2%)
  loops' own time  12.6 us (2%)
    psum x2, blocking collectives, shape_the_masks(): page = psum(page, k)  110 us
    dot_general x57, matrix products, contract(): lax.dot_general(left_op, right_op, (((left_dim,), (right_dim,)), ((), ())...  68 us
    psum x1, waiting for transfers between devices, local(): projected = lax.psum(partial_proj, 'col')  54 us
    psum x2, waiting for transfers between devices, shape_the_masks(): page = psum(page, k)  39.8 us
    all_to_all x1, waiting for transfers between devices, local(): lax.all_to_all(back_pairs, 'col', split_axis=0, concat_axis=0, tiled=True)  28.7 us
    reduce_sum x20, other arithmetic, transition_forward(): jnp.mean(centred * centred, axis=-1, keepdims=True) + 1e-05  23.1 us
    dot_general x12, matrix products, transition_forward(): result = jnp.dot(hidden_act, w_out, preferred_element_type=jnp.float32)  20.6 us
    reduce_sum x20, other arithmetic, transition_forward(): average = jnp.mean(start_z, axis=-1, keepdims=True)  19.2 us
  transfers between devices with their start and end apart: 6, of which 5 were waited for; matrix products, arithmetic and copies ran while one was open for 9% of the time, Pallas kernels for 0%

profile of v1, /device:TPU:1, one launch (start us, length us, event | category | flops | bytes accessed | tf_op | source)
XLA Modules:
  0.0 565.6 jit_solution(16017105605605874845)
XLA Ops:
  7.9 1.5 fusion.87
  13.8 1.9 gather_fusion.2
  21.9 7.6 %all-to-all-start.1 = ((bf16[16,2,256]{2,1,0:T(2,128)(2,1)}), bf16[16,2,256]{2,1,0:T(2,128)(2,1)S(1)}, u32[]{:S(2)}, u32[]{:S(2)}) async-start(bf16[16,2,256]{2,1,0:T(2,128)(2,1)} %reshape.938), calls=%async_computation.1 | async-start | bytes 32768 | tf_op jit(solution)/shard_map/all_to_all | solution.py:194
  30.6 10.0 %fusion.77 = s32[128]{0:T(128)S(1)} fusion(s32[128]{0:T(128)S(1)} %convert_reduce_fusion.1, s32[]{:T(128)} %bitcast.33, s32[]{:T(128)} %bitcast.34, s32[]{:T(128)} %bitcast.35, s32[]{:T(128)} %bitcast.36, s32[]{:T(128)} %bitcast.37, s32[]{:T(128)} %bitcast.39, s32[]{:T(128)} %bitcast.38, s32[]{:T(128)} %bitcast.16, s32[]{:T(128)} %bitcast.18, s32[]{:T(128)} %bitcast.20, ...), kind=kLoop, calls=%fused_computation.208 | loop fusion | flops 7296 | bytes 1092 | tf_op jit(solution)/shard_map/select_n | solution.py:202
  42.0 54.0 %all-reduce.8.cloned.1.call-done = f32[128,256]{1,0:T(8,128)} async-done(((f32[128,256]{1,0:T(8,128)}), f32[128,256]{1,0:T(8,128)}) %all-reduce.8.cloned.1.call-update) | async-done | bytes 131088 | tf_op jit(solution)/shard_map/psum | solution.py:121
  96.8 15.6 %all_gather.3 = bf16[1024,128]{1,0:T(8,128)(2,1)S(1)} all-gather(bf16[128,128]{1,0:T(8,128)(2,1)S(1)} %slice.95), channel_id=1, replica_groups=mesh['row'=8,'col'=16] {'row'}, dimensions={0}, use_global_device_ids=true | all-gather | bytes 294912 | tf_op jit(solution)/shard_map/all_gather | solution.py:125
  112.5 1.5 slice.72
  113.9 1.6 broadcast.784.clone
  115.5 64.0 %while.55 = (s32[]{:T(128)}, bf16[8,1024,128]{2,1,0:T(8,128)(2,1)}, s32[8]{0:T(128)S(1)}, bf16[128,64,128]{2,1,0:T(8,128)(2,1)}, f32[128,128]{1,0:T(8,128)}, /*i...) while((s32[]{:T(128)}, bf16[8,1024,128]{2,1,0:T(8,128)(2,1)}, ...), condition=%wide.region_6.7_spmd, body=%wide.region_3.6_spmd.sunk | while | flops 407897088 | bytes 11818179 | solution.py:145
  121.2 2.3 fusion.163
  126.7 1.4 multiply_reduce_fusion.5
  129.2 2.3 fusion.163
  137.2 2.3 fusion.163
  142.7 1.4 multiply_reduce_fusion.5
  145.2 2.3 fusion.163
  153.2 2.3 fusion.163
  158.7 1.4 multiply_reduce_fusion.5
  161.2 2.3 fusion.163
  166.7 1.4 multiply_reduce_fusion.5
  169.2 2.3 fusion.163
  177.2 2.3 fusion.163
  179.6 2.6 gather_fusion.3
  182.2 1.6 broadcast_select_fusion
  183.7 4.8 all-to-all-start
  189.2 22.2 %while.56 = (s32[]{:T(128)}, f32[128,64]{0,1:T(8,128)S(1)}, bf16[8,1024,128]{2,1,0:T(8,128)(2,1)S(1)}, bf16[8,1024,128]{2,1,0:T(8,128)(2,1)}, bf16[128,64]{0,1:T...) while((s32[]{:T(128)}, f32[128,64]{0,1:T(8,128)S(1)}, ...), condition=%wide.region_10.11_spmd.clone, body=%wide.region_7.10_spmd.clone.sunk | while | flops 51592192 | bytes 1995891 | solution.py:173
  211.5 9.9 %all-to-all-done = bf16[16,16,32,128]{3,2,1,0:T(8,128)(2,1)} async-done(((bf16[16,16,32,128]{3,2,1,0:T(8,128)(2,1)}), bf16[16,16,32,128]{3,2,1,0:T(8,128)(2,1)}, u32[]{:S(2)}, u32[]{:S(2)}) %all-to-all-start) | async-done | bytes 2097184 | tf_op jit(solution)/shard_map/all_to_all | solution.py:193
  221.4 2.4 gather_fusion.4
  223.8 45.5 %while.57 = (s32[]{:T(128)}, f32[128,1024]{1,0:T(8,128)}, f32[512,128]{1,0:T(8,128)S(1)}, f32[128,64]{0,1:T(8,128)S(1)}, bf16[4,1024,128]{2,1,0:T(8,128)(2,1)}, ...) while((s32[]{:T(128)}, f32[128,1024]{1,0:T(8,128)}, ...), condition=%wide.region_19.20_spmd.clone, body=%wide.region_12.19_spmd.clone.sunk | while | flops 1282874368 | bytes 39037144 | solution.py:216
  231.5 3.5 fusion.189
  242.8 3.7 fusion.189
  254.2 3.7 fusion.189
  265.6 3.7 fusion.189
  269.3 2.3 gather_fusion.7
  271.6 1.5 broadcast_select_fusion.1
  273.2 3.7 all-to-all-start.2
  277.9 28.7 %all-to-all-done.2 = bf16[16,16,32,128]{3,2,1,0:T(8,128)(2,1)S(1)} async-done(((bf16[16,16,32,128]{3,2,1,0:T(8,128)(2,1)}), bf16[16,16,32,128]{3,2,1,0:T(8,128)(2,1)S(1)}, u32[]{:S(2)}, u32[]{:S(2)}) %all-to-all-start.2) | async-done | bytes 2097184 | tf_op jit(solution)/shard_map/all_to_all | solution.py:226
  306.6 2.2 gather_fusion.8
  308.7 3.6 bitcast_select_fusion
  312.3 89.8 %while.58 = (s32[]{:T(128)}, f32[64,128]{1,0:T(8,128)S(1)}, bf16[8,16,64,128]{3,2,1,0:T(8,128)(2,1)}, f32[8,16,128]{2,1,0:T(8,128)}, bf16[8,1024,128]{2,1,0:T(8,...) while((s32[]{:T(128)}, f32[64,128]{1,0:T(8,128)S(1)}, ...), condition=%wide.region_27.28_spmd.clone, body=%wide.region_20.27_spmd.clone.sunk | while | flops 686169088 | bytes 20674808 | solution.py:250
  318.1 2.0 fusion.198
  320.1 1.4 fusion.199
  329.3 2.0 fusion.198
  331.3 1.4 fusion.199
  340.5 2.0 fusion.198
  342.5 1.4 fusion.199
  351.7 2.0 fusion.198
  353.8 1.4 fusion.199
  360.3 1.4 multiply_reduce_fusion.6
  362.9 2.0 fusion.198
  365.0 1.4 fusion.199
  374.2 2.0 fusion.198
  376.2 1.4 fusion.199
  382.8 1.4 multiply_reduce_fusion.6
  385.4 2.0 fusion.198
  387.4 1.4 fusion.199
  394.0 1.4 multiply_reduce_fusion.6
  396.6 2.0 fusion.198
  398.7 1.4 fusion.199
  404.1 56.7 %psum.70 = f32[128,64]{0,1:T(8,128)S(1)} all-reduce(f32[128,64]{0,1:T(8,128)S(1)} %get-tuple-element.223), channel_id=1, replica_groups=mesh['row'=8,'col'=16] {'col'}, use_global_device_ids=true, to_apply=%region_34.35 | all-reduce | flops 8192 | bytes 65536 | tf_op jit(solution)/shard_map/psum | solution.py:110
  460.8 30.5 %all-reduce.10.cloned.1.call-done = (f32[1024,256]{1,0:T(8,128)}, f32[128,1024]{1,0:T(8,128)}, f32[512,128]{1,0:T(8,128)}) async-done(((f32[1024,256]{1,0:T(8,128)}, f32[128,1024]{1,0:T(8,128)}, f32[512,128]{1,0:T(8,128)}), (f32[1024,256]{1,0:T(8,128)}, f32[128,1024]{1,0:T(8,128)}, f32[512,128]{1,0:T(8,128)})) %all-reduce.10.cloned.1.call-update) | async-done | bytes 1835024 | tf_op jit(solution)/shard_map/psum | solution.py:110
  491.3 53.4 %all-reduce.13 = (bf16[1024,256]{1,0:T(8,128)(2,1)S(1)}, f32[128,64]{0,1:T(8,128)S(1)}) all-reduce(f32[1024,256]{1,0:T(8,128)} %get-tuple-element.405, f32[128,64]{0,1:T(8,128)S(1)} %psum.70), channel_id=1, replica_groups=mesh['row'=8,'col'=16] {'row'}, use_global_device_ids=true, to_apply=%region_29.30 | all-reduce | flops 270336 | bytes 1638400 | tf_op jit(solution)/shard_map/psum | solution.py:110
  546.1 9.4 %all-reduce.12.cloned.1.call-done = (f32[128,1024]{1,0:T(8,128)}, f32[512,128]{1,0:T(8,128)}) async-done(((f32[128,1024]{1,0:T(8,128)}, f32[512,128]{1,0:T(8,128)}), (f32[128,1024]{1,0:T(8,128)}, f32[512,128]{1,0:T(8,128)})) %all-reduce.12.cloned.1.call-update) | async-done | bytes 786448 | tf_op jit(solution)/shard_map/psum | solution.py:110
  555.5 1.9 broadcast_multiply_fusion.7
  557.4 1.7 broadcast_multiply_fusion.8
  (446 shorter events, 158.4 us)
Async XLA Ops:
  7.2 0.7 copy-start
  7.2 6.6 %copy-start.1 = (s32[1,256]{1,0:T(1,128)S(1)}, s32[1,256]{1,0:T(1,128)}, u32[]{:S(2)}) copy-start(s32[1,256]{1,0:T(1,128)} %param.35) | copy-start | bytes 3076
  7.2 88.8 %all-reduce.8.cloned.1.call-start = ((), (), s32[]{:S(2)}) async-start(), calls=%async_computation.3 | async-start | bytes 262144 | tf_op jit(solution)/shard_map/psum | solution.py:121
  13.8 3.7 copy-start.10
  13.8 5.6 copy-start.12
  20.2 95.3 %copy-start.2 = (bf16[128,1024]{1,0:T(8,128)(2,1)S(1)}, bf16[128,1024]{1,0:T(8,128)(2,1)}, u32[]{:S(2)}) copy-start(bf16[128,1024]{1,0:T(8,128)(2,1)} %param.26) | copy-start | bytes 786436
  20.2 95.3 %copy-start.9 = (f32[128]{0:T(128)S(1)}, f32[128]{0:T(128)}, u32[]{:S(2)}) copy-start(f32[128]{0:T(128)} %param.25) | copy-start | bytes 1540
  21.9 19.1 %all-to-all-start.1 = ((bf16[16,2,256]{2,1,0:T(2,128)(2,1)}), bf16[16,2,256]{2,1,0:T(2,128)(2,1)S(1)}, u32[]{:S(2)}, u32[]{:S(2)}) async-start(bf16[16,2,256]{2,1,0:T(2,128)(2,1)} %reshape.938), calls=%async_computation.1 | async-start | bytes 32768 | tf_op jit(solution)/shard_map/all_to_all | solution.py:194
  183.7 37.6 %all-to-all-start = ((bf16[16,16,32,128]{3,2,1,0:T(8,128)(2,1)}), bf16[16,16,32,128]{3,2,1,0:T(8,128)(2,1)}, u32[]{:S(2)}, u32[]{:S(2)}) async-start(bf16[16,16,32,128]{3,2,1,0:T(8,128)(2,1)} %broadcast_select_fusion), calls=%async_computation | async-start | bytes 4194304 | tf_op jit(solution)/shard_map/all_to_all | solution.py:193
  188.5 0.7 copy-start.8
  211.4 9.9 %copy-start.4 = (bf16[8,1024,128]{2,1,0:T(8,128)(2,1)}, bf16[8,1024,128]{2,1,0:T(8,128)(2,1)S(1)}, u32[]{:S(2)}) copy-start(bf16[8,1024,128]{2,1,0:T(8,128)(2,1)S(1)} %get-tuple-element.217) | copy-start | bytes 6291460
  211.4 12.3 %copy-start.5 = (bf16[128,1024]{1,0:T(8,128)(2,1)S(1)}, bf16[128,1024]{1,0:T(8,128)(2,1)}, u32[]{:S(2)}) copy-start(bf16[128,1024]{1,0:T(8,128)(2,1)} %param.29) | copy-start | bytes 786436
  211.5 12.3 %copy-start.7 = (bf16[512,128]{1,0:T(8,128)(2,1)S(1)}, bf16[512,128]{1,0:T(8,128)(2,1)}, u32[]{:S(2)}) copy-start(bf16[512,128]{1,0:T(8,128)(2,1)} %param.30) | copy-start | bytes 393220
  211.5 12.3 %copy-start.11 = (f32[128]{0:T(128)S(1)}, f32[128]{0:T(128)}, u32[]{:S(2)}) copy-start(f32[128]{0:T(128)} %param.28) | copy-start | bytes 1540
  228.1 1.4 copy-start.13
  228.1 1.4 copy-start.14
  239.4 1.4 copy-start.13
  239.4 1.4 copy-start.14
  250.8 1.4 copy-start.13
  250.8 1.4 copy-start.14
  262.2 1.4 copy-start.13
  262.2 1.4 copy-start.14
  269.3 2.3 copy-start.3
  273.2 33.4 %all-to-all-start.2 = ((bf16[16,16,32,128]{3,2,1,0:T(8,128)(2,1)}), bf16[16,16,32,128]{3,2,1,0:T(8,128)(2,1)S(1)}, u32[]{:S(2)}, u32[]{:S(2)}) async-start(bf16[16,16,32,128]{3,2,1,0:T(8,128)(2,1)} %broadcast_select_fusion.1), calls=%async_computation.2 | async-start | bytes 4194304 | tf_op jit(solution)/shard_map/all_to_all | solution.py:226
  276.9 214.4 %all-reduce.10.cloned.1.call-start = ((), (), s32[]{:S(2)}) async-start(), calls=%async_computation.4 | async-start | bytes 3670016 | tf_op jit(solution)/shard_map/psum | solution.py:110
  403.0 1.0 copy-start.6
  404.1 151.4 %all-reduce.12.cloned.1.call-start = ((), (), s32[]{:S(2)}) async-start(), calls=%async_computation.5 | async-start | bytes 1572864 | tf_op jit(solution)/shard_map/psum | solution.py:110
Sparse Core Ops, SparseCore 0:
  11.8 84.1 all-reduce.7
  404.2 87.0 all-reduce.9
  493.7 61.6 all-reduce.11
